TPU v7x, 32 devices: a whole 2x2x4 slice. The times are simulated.
32 devices in a mesh: round: 2 (over x), brick: 16 (over z, y, core).
Axes of the slice: x: 2, y: 2, z: 4, core: 2. Of those that a mesh axis runs over, the one named last changes fastest.
Arguments:
- image: bfloat16 [2, 128, 4, 32, 8, 128], P('round', 'brick'), may hold values from -60 to 60
- shifts: int32 [2, 128], P('round', 'brick'), may hold values from -24 to 24, as said below
- fractions: float32 [2, 128], P('round', 'brick'), may hold values from 0 to 1
- valid: int32 [128], replicated, may hold values from 0 to 1, as said below
Outputs:
- spots: bfloat16 [2, 2, 64, 4, 32, 8, 128], P(None, 'round', 'brick')
Inputs may be any that keep to these rules, and one draw needn't show every extreme that they name: `shifts`: in every round, the last brick of each aligned block of 8 bricks has a shift between minus 24 and minus half of 24 (rounded down), and the first brick of each such block a shift between half of 24 (rounded down) and 24. `valid`: the first and the last brick of each aligned block of 8 bricks hold tissue.
All inputs are finite; a program needn't handle non-finite values.
Results may differ from a plain program's by a relative error of at most 0.0055.
Values may be sent and summed in bfloat16 or wider, within the bound.
No kernel may reach another device: no remote copies, remote signals or barrier semaphores. Data moves between devices by JAX's collectives and lax.ppermute only.
A program may use at most 128 MiB of HBM per device.

v0:
```python
import jax
import jax.numpy as jnp
from jax import lax
from jax.sharding import PartitionSpec as P

SMAX = 24


sigma_spot = 1.5


def with_halo(cells, sides, width):
    for axis, dim in sides:
        count = lax.axis_size(axis)
        ends = count - 1
        head = lax.slice_in_dim(cells, 0, width, axis=dim)
        tail = lax.slice_in_dim(cells, cells.shape[dim] - width, cells.shape[dim], axis=dim)
        cells = jnp.concatenate(
            [
                lax.ppermute(tail, axis, [(i, (i + 1) % count) for i in range(ends)]),
                cells,
                lax.ppermute(head, axis, [((i + 1) % count, i) for i in range(ends)]),
            ],
            axis=dim,
        )
    return cells


def kernel_tables(count):
    index = jnp.arange(count, dtype=jnp.float32)
    offset = index[:, None] - index[None, :]
    smooth = jnp.exp(-offset * offset / (2.0 * sigma_spot * sigma_spot)) / (
        2.5066282746310002 * sigma_spot
    )
    smooth = jnp.where(jnp.abs(offset) < 4.0 * sigma_spot, smooth, jnp.float32(0.0))
    curve = (offset * offset / sigma_spot**4 - 1.0 / sigma_spot**2) * smooth
    return (smooth, curve)


def spot_filter(field):
    values = field.astype(jnp.float32)
    depth, height, width = field.shape[-3:]
    gauss_z, curve_z = kernel_tables(depth)
    gauss_y, curve_y = kernel_tables(height)
    gauss_x, curve_x = kernel_tables(width)
    high = lax.Precision.HIGHEST
    along_x = jnp.einsum("...x,wx->...w", values, gauss_x, precision=high)
    bent_x = jnp.einsum("...x,wx->...w", values, curve_x, precision=high)
    plain_y = jnp.einsum("...yx,vy->...vx", along_x, gauss_y, precision=high)
    bent_y = jnp.einsum("...yx,vy->...vx", along_x, curve_y, precision=high)
    mixed_y = jnp.einsum("...yx,vy->...vx", bent_x, gauss_y, precision=high)
    outer = jnp.einsum("...zyx,wz->...wyx", mixed_y + bent_y, gauss_z, precision=high)
    outer = outer + jnp.einsum("...zyx,wz->...wyx", plain_y, curve_z, precision=high)
    return (-(sigma_spot * sigma_spot) * outer).astype(jnp.bfloat16)


def on_device(image, shifts, fractions, valid):
    layer = image[0]
    bricks_here, channels, depth, height, width = layer.shape
    rounds = lax.axis_size("round")
    brick_index = lax.axis_index("brick")
    round_index = lax.axis_index("round")
    reach = SMAX + 1
    own_valid = lax.dynamic_slice_in_dim(valid, brick_index * bricks_here, bricks_here)
    masked = layer * own_valid.astype(jnp.bfloat16)[:, None, None, None, None]
    strip = jnp.moveaxis(masked, 0, 3).reshape(channels, depth, height, bricks_here * width)
    padded = with_halo(strip, (("brick", 3),), reach)
    offsets = jnp.arange(bricks_here, dtype=jnp.int32) * width + reach - shifts[0] - 1

    def one_brick(start, fraction):
        window = lax.dynamic_slice_in_dim(padded, start, width + 1, 3).astype(jnp.float32)
        return ((1.0 - fraction) * window[..., 1:] + fraction * window[..., :-1]).astype(
            jnp.bfloat16
        )

    shifted = jax.vmap(one_brick)(offsets, fractions[0])
    filtered = spot_filter(shifted)
    magnitude = jnp.sum(jnp.abs(filtered.astype(jnp.float32)), axis=(2, 3, 4))
    sums = jnp.sum(magnitude * own_valid.astype(jnp.float32)[:, None], axis=0)
    selector = (jnp.arange(rounds, dtype=jnp.int32) == round_index).astype(jnp.float32)
    stats = selector[:, None] * sums[None, :]
    moved = lax.all_to_all(filtered[None], "round", split_axis=1, concat_axis=0, tiled=True)
    totals = lax.psum(stats, ("round", "brick"))
    count = jnp.maximum(jnp.sum(valid).astype(jnp.float32), 1.0)
    scale = totals / (count * depth * height * width) + 1e-06
    ratio = moved.astype(jnp.float32) / scale[:, None, :, None, None, None]
    energy = jnp.mean(ratio * ratio, axis=(0, 2), keepdims=True)
    normed = (ratio / jnp.sqrt(energy + 1.0)).astype(jnp.bfloat16)
    return normed[:, None]


def solution(mesh):
    in_specs = (
        P("round", "brick", None, None, None, None),
        P("round", "brick"),
        P("round", "brick"),
        P(),
    )
    out_specs = P(None, "round", "brick", None, None, None, None)
    return jax.shard_map(
        on_device, mesh=mesh, in_specs=in_specs, out_specs=out_specs, check_vma=False
    )
```

profile of v0, /device:TPU:0, one launch (start us, length us, event | category | flops | bytes accessed | tf_op | source)
XLA Modules:
  0.0 157.6 jit_solution(13415538500700962001)
XLA Ops:
  0.0 0.0 copy-start.2
  0.0 0.0 copy-start
  0.0 0.8 dynamic-slice_convert_fusion
  0.8 2.3 %copy_bitcast_fusion = bf16[4,32,8,1024]{3,2,1,0:T(8,128)(2,1)S(1)} fusion(bf16[1,8,4,32,8,128]{5,4,3,2,1,0:T(8,128)(2,1)} %param.4, bf16[8]{0:T(256)(128)(2,1)S(1)} %get-tuple-element.8), kind=kLoop, calls=%fused_computation.18 | loop fusion | flops 1048576 | bytes 4194320 | tf_op jit(solution)/shard_map/reshape | solution.py:66
  3.0 0.2 fusion.120
  3.2 2.4 %collective-permute-start = (bf16[4,32,8,25]{3,2,1,0:T(8,128)(2,1)S(1)}, bf16[4,32,8,25]{3,2,1,0:T(8,128)(2,1)S(1)}, u32[]{:S(2)}, u32[]{:S(2)}) collective-permute-start(bf16[4,32,8,25]{3,2,1,0:T(8,128)(2,1)S(1)} %get-tuple-element.6), channel_id=1, source_target_pairs={{0,1},{1,2},{2,3},{3,4},{4,5},{5,6},{6,7},{7,8},{8,9},{9,10},{10,1... | collective-permute-start | bytes 153608 | tf_op jit(solution)/shard_map/ppermute | solution.py:20
  5.6 1.3 collective-permute-start.1
  6.9 0.0 copy-done.2
  7.0 0.0 copy-done
  7.0 0.0 collective-permute-done
  7.0 4.2 %collective-permute-done.1 = bf16[4,32,8,25]{3,2,1,0:T(8,128)(2,1)S(1)} collective-permute-done((bf16[4,32,8,25]{3,2,1,0:T(8,128)(2,1)S(1)}, bf16[4,32,8,25]{3,2,1,0:T(8,128)(2,1)S(1)}, u32[]{:S(2)}, u32[]{:S(2)}) %collective-permute-start.1) | collective-permute-done | bytes 51232 | tf_op jit(solution)/shard_map/ppermute | solution.py:22
  11.2 4.0 %concatenate.6 = bf16[4,32,8,1074]{3,2,1,0:T(8,128)(2,1)} concatenate(bf16[4,32,8,25]{3,2,1,0:T(8,128)(2,1)S(1)} %collective-permute-done, bf16[4,32,8,1024]{3,2,1,0:T(8,128)(2,1)S(1)} %copy_bitcast_fusion, bf16[4,32,8,25]{3,2,1,0:T(8,128)(2,1)S(1)} %collective-permute-done.1), dimensions={3} | concatenate | bytes 4399104 | tf_op jit(solution)/shard_map/concatenate | solution.py:18
  15.2 16.7 %copy.56 = bf16[4,32,8,1074]{1,2,0,3:T(8,128)(2,1)} copy(bf16[4,32,8,1074]{3,2,1,0:T(8,128)(2,1)} %concatenate.6) | data formatting | bytes 4399104 | tf_op jit(solution)/shard_map/concatenate | solution.py:18
  31.9 8.3 %gather_fusion = bf16[8,4,32,8,129]{2,3,1,4,0:T(8,128)(2,1)} fusion(bf16[4,32,8,1074]{1,2,0,3:T(8,128)(2,1)} %copy.56, s32[8]{0:T(128)S(1)} %shift-left_bitcast_fusion), kind=kCustom, calls=%fused_computation | custom fusion | bytes 4227200 | tf_op jit(solution)/shard_map/vmap()/gather | solution.py:71
  40.2 13.0 %copy.57 = bf16[8,4,32,8,129]{4,3,2,1,0:T(8,128)(2,1)} copy(bf16[8,4,32,8,129]{2,3,1,4,0:T(8,128)(2,1)} %gather_fusion) | data formatting | bytes 4227072 | tf_op jit(solution)/shard_map/vmap()/gather | solution.py:71
  53.1 3.2 %convert_element_type.59 = f32[8,4,32,8,129]{4,3,2,1,0:T(8,128)S(1)} convert(bf16[8,4,32,8,129]{4,3,2,1,0:T(8,128)(2,1)} %copy.57) | non-fusion elementwise | flops 1056768 | bytes 6340608 | tf_op jit(solution)/shard_map/vmap()/convert_element_type | solution.py:71
  56.4 1.5 fusion.1
  57.9 1.8 %fusion.14 = f32[8,4,32,8,128]{4,3,2,1,0:T(8,128)S(1)} fusion(bf16[8,4,32,8,128]{4,3,2,1,0:T(8,128)(2,1)S(1)} %fusion.1), kind=kOutput, calls=%fused_computation.25 | convolution fusion | flops 1610743808 | bytes 6291456 | tf_op jit(solution)/shard_map/...x,wx->...w/dot_general | solution.py:47
  59.7 1.8 %fusion.16 = f32[8,4,32,8,128]{4,3,2,1,0:T(8,128)S(1)} fusion(bf16[8,4,32,8,128]{4,3,2,1,0:T(8,128)(2,1)S(1)} %fusion.1), kind=kOutput, calls=%fused_computation.27 | convolution fusion | flops 1610809344 | bytes 6291456 | tf_op jit(solution)/shard_map/...x,wx->...w/dot_general | solution.py:48
  61.6 3.6 %fusion.62 = f32[8,8,4,32,128]{4,0,3,2,1:T(8,128)S(1)} fusion(f32[8,4,32,8,128]{4,3,2,1,0:T(8,128)S(1)} %fusion.16), kind=kOutput, calls=%fused_computation.75 | convolution fusion | flops 100663808 | bytes 8388608 | tf_op jit(solution)/shard_map/...yx,vy->...vx/dot_general | solution.py:51
  65.2 3.9 %convolution_bitcast_fusion = f32[8,4,32,8,128]{4,3,2,1,0:T(8,128)S(1)} fusion(f32[8,4,32,8,128]{4,3,2,1,0:T(8,128)S(1)} %fusion.14), kind=kOutput, calls=%fused_computation.15 | convolution fusion | flops 100663808 | bytes 8388608 | tf_op jit(solution)/shard_map/...yx,vy->...vx/dot_general | solution.py:49
  69.1 3.6 %add_bitcast_fusion = f32[8,4,32,8,128]{4,3,2,1,0:T(8,128)S(1)} fusion(f32[8,8,4,32,128]{4,0,3,2,1:T(8,128)S(1)} %fusion.62, f32[8,4,32,8,128]{4,3,2,1,0:T(8,128)S(1)} %fusion.14), kind=kOutput, calls=%fused_computation.14 | convolution fusion | flops 101712640 | bytes 12582912 | tf_op jit(solution)/shard_map/...yx,vy->...vx/dot_general | solution.py:50
  72.7 3.8 %fusion.3 = f32[32,8,4,8,128]{4,0,3,2,1:T(8,128)S(1)} fusion(f32[8,4,32,8,128]{4,3,2,1,0:T(8,128)S(1)} %convolution_bitcast_fusion), kind=kOutput, calls=%fused_computation.8 | convolution fusion | flops 402665472 | bytes 8388608 | tf_op jit(solution)/shard_map/...zyx,wz->...wyx/dot_general | solution.py:53
  76.6 5.3 %abs_reduce_fusion = (f32[8,4]{1,0:T(8,128)S(1)}, bf16[32,8,4,8,128]{4,0,3,2,1:T(8,128)(2,1)}) fusion(f32[32,8,4,8,128]{4,0,3,2,1:T(8,128)S(1)} %fusion.3, f32[8,4,32,8,128]{4,3,2,1,0:T(8,128)S(1)} %add_bitcast_fusion), kind=kOutput, calls=%fused_computation.12 | convolution fusion | flops 408952800 | bytes 10485888 | tf_op jit(solution)/shard_map/...zyx,wz->...wyx/dot_general | solution.py:52
  81.8 0.0 copy-start.1
  81.8 3.9 %all-to-all-start = ((bf16[1,8,4,32,8,128]{5,3,4,2,0,1:T(8,128)(2,1)}), bf16[1,8,4,32,8,128]{5,3,4,2,0,1:T(8,128)(2,1)S(1)}, u32[]{:S(2)}, u32[]{:S(2)}) async-start(bf16[1,8,4,32,8,128]{5,3,4,2,0,1:T(8,128)(2,1)} %bitcast.76), calls=%async_computation | async-start | bytes 4194304 | tf_op jit(solution)/shard_map/all_to_all | solution.py:82
  85.8 0.0 copy-done.1
  85.8 0.7 reduce_sum.45
  87.2 0.1 multiply_reduce_fusion
  87.3 0.1 broadcast_multiply_fusion
  87.3 61.2 %psum.7 = f32[2,4]{1,0:T(2,128)S(1)} all-reduce(f32[2,4]{1,0:T(2,128)S(1)} %broadcast_multiply_fusion), channel_id=1, replica_groups=mesh['round'=2,'brick'=16] {'round','brick'}, use_global_device_ids=true, to_apply=%region_2.3 | all-reduce | flops 8 | bytes 64 | tf_op jit(solution)/shard_map/psum | solution.py:83
  148.6 0.0 all-to-all-done
  148.6 0.7 bitcast_reduce_fusion
  149.2 0.9 reduce_sum.48
  150.1 1.2 add_sqrt_fusion
  151.3 0.3 copy.65
  151.7 0.6 convert.1
  152.2 5.3 %fusion.2 = bf16[2,1,4,4,32,8,128]{6,5,4,3,2,1,0:T(8,128)(2,1)} fusion(f32[2,1,4,4,32,8,128]{6,4,5,3,2,0,1:T(8,128)S(1)} %convert.1, f32[4,32,8,128]{3,2,1,0:T(8,128)S(1)} %copy.65, f32[2,4]{1,0:T(2,128)S(1)} %divide_add_fusion), kind=kLoop, calls=%fused_computation.7 | loop fusion | flops 3145728 | bytes 6815776 | tf_op jit(solution)/shard_map/convert_element_type | solution.py:88
  (5 shorter events, 0.0 us)
Async XLA Ops:
  0.0 6.9 %copy-start.2 = (s32[1,8]{1,0:T(1,128)S(1)}, s32[1,8]{1,0:T(1,128)}, u32[]{:S(2)}) copy-start(s32[1,8]{1,0:T(1,128)} %param.5) | copy-start | bytes 100
  0.0 7.0 %copy-start = (f32[1,8]{1,0:T(1,128)S(1)}, f32[1,8]{1,0:T(1,128)}, u32[]{:S(2)}) copy-start(f32[1,8]{1,0:T(1,128)} %param.6) | copy-start | bytes 100
  3.2 3.8 %collective-permute-start = (bf16[4,32,8,25]{3,2,1,0:T(8,128)(2,1)S(1)}, bf16[4,32,8,25]{3,2,1,0:T(8,128)(2,1)S(1)}, u32[]{:S(2)}, u32[]{:S(2)}) collective-permute-start(bf16[4,32,8,25]{3,2,1,0:T(8,128)(2,1)S(1)} %get-tuple-element.6), channel_id=1, source_target_pairs={{0,1},{1,2},{2,3},{3,4},{4,5},{5,6},{6,7},{7,8},{8,9},{9,10},{10,1... | collective-permute-start | bytes 153608 | tf_op jit(solution)/shard_map/ppermute | solution.py:20
  5.6 5.5 %collective-permute-start.1 = (bf16[4,32,8,25]{3,2,1,0:T(8,128)(2,1)S(1)}, bf16[4,32,8,25]{3,2,1,0:T(8,128)(2,1)S(1)}, u32[]{:S(2)}, u32[]{:S(2)}) collective-permute-start(bf16[4,32,8,25]{3,2,1,0:T(8,128)(2,1)S(1)} %get-tuple-element.5), channel_id=1, source_target_pairs={{1,0},{2,1},{3,2},{4,3},{5,4},{6,5},{7,6},{8,7},{9,8},{10,9},{11,1... | collective-permute-start | bytes 153608 | tf_op jit(solution)/shard_map/ppermute | solution.py:22
  81.8 3.9 %copy-start.1 = (s32[128]{0:T(128)S(1)}, s32[128]{0:T(128)}, u32[]{:S(2)}) copy-start(s32[128]{0:T(128)} %param.7) | copy-start | bytes 1540
  81.8 66.7 %all-to-all-start = ((bf16[1,8,4,32,8,128]{5,3,4,2,0,1:T(8,128)(2,1)}), bf16[1,8,4,32,8,128]{5,3,4,2,0,1:T(8,128)(2,1)S(1)}, u32[]{:S(2)}, u32[]{:S(2)}) async-start(bf16[1,8,4,32,8,128]{5,3,4,2,0,1:T(8,128)(2,1)} %bitcast.76), calls=%async_computation | async-start | bytes 4194304 | tf_op jit(solution)/shard_map/all_to_all | solution.py:82
where the time goes:
time: 158 us
  blocking collectives  61.2 us (39%)
  local copies, waits for them, and re-layouts  42.4 us (27%)
  matrix products  23.9 us (15%)
  other arithmetic  17.3 us (11%)
  starting transfers between devices  7.6 us (5%)
  waiting for transfers between devices  4.18 us (3%)
    psum x1, blocking collectives, on_device(): totals = lax.psum(stats, ('round', 'brick'))  61.2 us
    gather x2, local copies, waits for them, and re-layouts, one_brick(): lax.dynamic_slice_in_dim(padded, start, width + 1, 3).astype(jnp.float32)  21.2 us
    concatenate x2, local copies, waits for them, and re-layouts, with_halo(): jnp.concatenate([lax.ppermute(tail, axis, [(i, (i + 1) % count) for i in...  20.7 us
    convert_element_type x1, other arithmetic, on_device(): normed = (ratio / jnp.sqrt(energy + 1.0)).astype(jnp.bfloat16)  5.33 us
    dot_general x1, matrix products, spot_filter(): jnp.einsum('...zyx,wz->...wyx', mixed_y + bent_y, gauss_z, precision=high)  5.29 us
    ppermute x1, waiting for transfers between devices, with_halo(): lax.ppermute(head, axis, [((i + 1) % count, i) for i in range(ends)])  4.18 us
    all_to_all x1, starting transfers between devices, on_device(): lax.all_to_all(filtered[None], 'round', split_axis=1, concat_axis=0, tile...  3.9 us
    dot_general x1, matrix products, spot_filter(): plain_y = jnp.einsum('...yx,vy->...vx', along_x, gauss_y, precision=high)  3.87 us
  transfers between devices with their start and end apart: 3, of which 1 were waited for; matrix products, arithmetic and copies ran while one was open for 1% of the time, Pallas kernels for 0%

commit v1 on v0

v1 whole, which is shorter than its diff:
```python
import functools

import jax
import jax.numpy as jnp
import numpy as np
from jax import lax
from jax.experimental import pallas as pl
from jax.experimental.pallas import tpu as pltpu
from jax.sharding import PartitionSpec as P

SMAX = 24

sigma_spot = 1.5

BF = jnp.bfloat16
F32 = jnp.float32
VMEM = pl.BlockSpec(memory_space=pltpu.VMEM)
SMEM = pl.BlockSpec(memory_space=pltpu.SMEM)


def kernel_tables(count):
    index = np.arange(count, dtype=np.float64)
    offset = index[:, None] - index[None, :]
    smooth = np.exp(-offset * offset / (2.0 * sigma_spot * sigma_spot)) / (
        2.5066282746310002 * sigma_spot
    )
    smooth = np.where(np.abs(offset) < 4.0 * sigma_spot, smooth, 0.0)
    curve = (offset * offset / sigma_spot**4 - 1.0 / sigma_spot**2) * smooth
    return smooth, curve


def split(table):
    table = np.asarray(table, np.float32)
    high = table.astype(BF)
    low = (table - high.astype(np.float32)).astype(BF)
    return np.stack([high, low])


def plane_tables(depth, height):
    gauss_z, curve_z = kernel_tables(depth)
    gauss_y, curve_y = kernel_tables(height)
    factor = -(sigma_spot * sigma_spot)
    with_bent = np.kron(gauss_z, gauss_y)
    with_smooth = np.kron(gauss_z, curve_y) + np.kron(curve_z, gauss_y)
    return split(factor * np.concatenate([with_bent, with_smooth], axis=0))


def line_tables(width):
    gauss_x, curve_x = kernel_tables(width)
    return np.stack([np.tile(t.T, (2, 1)) for t in (curve_x, gauss_x)]).astype(np.float32)


def lanes_of(shape):
    return lax.broadcasted_iota(jnp.int32, shape, len(shape) - 1)


def pack_kernel(valid_ref, img_ref, tail_ref, head_ref):
    bricks, channels, plane, width = img_ref.shape
    slot = width // channels
    first = lax.axis_index("brick") * bricks
    lane = lanes_of((plane, width))

    def pack(brick, at):
        row = jnp.zeros((plane, width), F32)
        for c in range(channels):
            data = img_ref[brick, c].astype(F32)
            amount = (c * slot - at) % width
            moved = pltpu.roll(data, amount, 1) if amount else data
            row = jnp.where(lane // slot == c, moved, row)
        return (row * valid_ref[first + brick].astype(F32)).astype(BF)

    tail_ref[...] = pack(bricks - 1, width - slot)
    head_ref[...] = pack(0, 0)


def filter_kernel(picks, edge, first_call, last_call, *refs):
    shift_ref, frac_ref, valid_ref, img_ref, plane_ref, line_ref = refs[:6]
    refs = refs[6:]
    if edge:
        tail_ref, head_ref = refs[:2]
        refs = refs[2:]
    if not first_call:
        sums_ref, refs = refs[0], refs[1:]
    out_ref, stat_ref = refs
    bricks, channels, plane, width = img_ref.shape
    slot = width // channels
    first = lax.axis_index("brick") * bricks
    rank = lax.axis_index("round")
    lane = lanes_of((1, width))
    totals = [jnp.zeros((8, width), F32) for _ in range(channels)]
    for n, pick in enumerate(picks):
        b = pick(rank)
        s = shift_ref[0, b]
        f = frac_ref[0, b]
        right = s >= 0
        nb = jnp.where(right, b - 1, b + 1)
        nb_in = jnp.clip(nb, 0, bricks - 1)
        own_valid = valid_ref[first + b].astype(F32)
        nb_valid = valid_ref[jnp.clip(first + nb, 0, valid_ref.shape[0] - 1)].astype(F32)
        if edge:
            nb_valid = jnp.where(nb == nb_in, nb_valid, 1.0)
        low0, high0 = jnp.where(right, 0, -s), jnp.where(right, width - s, width)
        low1, high1 = jnp.where(right, 0, -s - 1), jnp.where(right, width - s - 1, width)
        own0 = (lane >= low0) & (lane < high0)
        own1 = (lane >= low1) & (lane < high1)
        gain0 = (1.0 - f) * jnp.where(own0, own_valid, nb_valid)
        gain1 = f * jnp.where(own1, own_valid, nb_valid)
        own0, own1 = (jnp.broadcast_to(m, (plane, width)) for m in (own0, own1))
        parts = []
        for c in range(channels):
            own = img_ref[b, c].astype(F32)
            other = img_ref[nb_in, c].astype(F32)
            if edge:
                before = pltpu.roll(tail_ref[...].astype(F32), (width - slot - c * slot) % width, 1)
                after = head_ref[...].astype(F32)
                if c:
                    after = pltpu.roll(after, (width - c * slot) % width, 1)
                other = jnp.where(nb < 0, before, jnp.where(nb >= bricks, after, other))
            here = jnp.where(own0, own, other) * gain0
            there = jnp.where(own1, own, other) * gain1
            parts.append((here + pltpu.roll(there, 1, 1)).astype(BF))
        field = jnp.concatenate(parts, axis=1)
        dot = functools.partial(jnp.dot, preferred_element_type=F32)
        mixed = dot(plane_ref[0], field) + dot(plane_ref[1], field)
        turn = jnp.where(s < 0, s + width, s)
        line = jnp.concatenate([line_ref[k, pl.ds(turn, width), :] for k in range(2)], axis=0)
        line_high = line.astype(BF)
        line_low = (line - line_high.astype(F32)).astype(BF)
        for c in range(channels):
            wide = jnp.concatenate(
                [mixed[k * plane : (k + 1) * plane, c * width : (c + 1) * width] for k in range(2)],
                axis=1,
            )
            wide_high = wide.astype(BF)
            wide_low = (wide - wide_high.astype(F32)).astype(BF)
            result = dot(wide_high, line_high) + dot(wide_high, line_low) + dot(wide_low, line_high)
            result = result.astype(BF)
            out_ref[n, c] = result
            size = jnp.abs(result.astype(F32)).reshape(plane // 8, 8, width)
            totals[c] = totals[c] + jnp.sum(size, axis=0) * own_valid
    if not first_call:
        totals = [totals[c] + sums_ref[c] for c in range(channels)]
    if last_call:
        row = lax.broadcasted_iota(jnp.int32, (8, width), 0)
        packed = jnp.zeros((8, width), F32)
        for c in range(channels):
            packed = jnp.where(row == c, jnp.sum(totals[c]), packed)
        stat_ref[...] = packed
    else:
        for c in range(channels):
            stat_ref[c] = totals[c]


def norm_kernel(rounds, places, *refs):
    valid_ref, own_ref = refs[:2]
    stat_refs = refs[2 : 2 + rounds]
    chunk_refs = refs[2 + rounds : -1]
    out_ref = refs[-1]
    quota, channels, plane, width = own_ref.shape
    rank = lax.axis_index("round")
    count = jnp.maximum(jnp.sum(valid_ref[...]).astype(F32), 1.0)
    inverse = []
    for d in range(rounds):
        scale = stat_refs[d][...] / (count * (plane * width)) + 1e-06
        inverse.append(1.0 / scale)
    for j in range(quota):
        pos = jnp.where(rank == 0, quota - 1 - j, j)
        energy = jnp.zeros((plane, width), F32)
        values = []
        for d in range(rounds):
            for c in range(channels):
                data = own_ref[pos, c] if d == 0 else chunk_refs[places[d, j]][0, c]
                ratio = data.astype(F32) * inverse[d][c : c + 1, :]
                energy = energy + ratio * ratio
                values.append(ratio)
        factor = lax.rsqrt(energy * (1.0 / (rounds * channels)) + 1.0)
        for d in range(rounds):
            slot = jnp.where(rank >= d, rank - d, rank - d + rounds)
            for c in range(channels):
                out_ref[slot, 0, pos, c] = (values[d * channels + c] * factor).astype(BF)


def on_device(image, shifts, fractions, valid):
    _, bricks, channels, depth, height, width = image.shape
    plane = depth * height
    rounds = lax.axis_size("round")
    count = lax.axis_size("brick")
    quota = bricks // rounds
    img = image.reshape(bricks, channels, plane, width)
    plane_table = jnp.asarray(plane_tables(depth, height))
    line_table = jnp.asarray(line_tables(width))
    shape = jax.ShapeDtypeStruct

    tail, head = pl.pallas_call(
        pack_kernel,
        in_specs=[SMEM, VMEM],
        out_specs=[VMEM, VMEM],
        out_shape=[shape((plane, width), BF)] * 2,
        name="pack",
    )(valid, img)
    ends = count - 1
    before = lax.ppermute(tail, "brick", [(i, i + 1) for i in range(ends)])
    after = lax.ppermute(head, "brick", [(i + 1, i) for i in range(ends)])

    def pick_for(d, j):
        def pick(rank):
            target = (rank + d) % rounds
            return target * quota + jnp.where(target == 0, quota - 1 - j, j)

        return pick

    def own_pick(j):
        return lambda rank: rank * quota + j

    sums = None

    def filtered(picks, edge, last, sums):
        ins = [shifts, fractions, valid, img, plane_table, line_table]
        specs = [SMEM, SMEM, SMEM, VMEM, VMEM, VMEM]
        if edge:
            ins += [before, after]
            specs += [VMEM, VMEM]
        if sums is not None:
            ins.append(sums)
            specs.append(VMEM)
        stat = shape((8, width), F32) if last else shape((channels, 8, width), F32)
        return pl.pallas_call(
            functools.partial(filter_kernel, picks, edge, sums is None, last),
            in_specs=specs,
            out_specs=[VMEM, VMEM],
            out_shape=[shape((len(picks), channels, plane, width), BF), stat],
            name=f"filter{len(picks)}",
        )(*ins)

    places = {}
    chunks = []
    for j in range(quota):
        for d in range(1, rounds):
            edge = j == quota - 1
            part, sums = filtered([pick_for(d, j)], edge, False, sums)
            places[d, j] = len(chunks)
            chunks.append(lax.ppermute(part, "round", [(i, (i + d) % rounds) for i in range(rounds)]))
    own, stat = filtered([own_pick(j) for j in range(quota)], True, True, sums)

    step = 1
    while step < count:
        stat = stat + lax.ppermute(stat, "brick", [(i, i ^ step) for i in range(count)])
        step *= 2
    stats = [stat]
    for d in range(1, rounds):
        stats.append(lax.ppermute(stat, "round", [(i, (i + d) % rounds) for i in range(rounds)]))

    out = pl.pallas_call(
        functools.partial(norm_kernel, rounds, places),
        in_specs=[VMEM] * (2 + rounds + len(chunks)),
        out_specs=VMEM,
        out_shape=shape((rounds, 1, quota, channels, plane, width), BF),
        name="norm",
    )(valid.reshape(1, -1), own, *stats, *chunks)
    return out.reshape(rounds, 1, quota, channels, depth, height, width)


def solution(mesh):
    in_specs = (
        P("round", "brick", None, None, None, None),
        P("round", "brick"),
        P("round", "brick"),
        P(),
    )
    out_specs = P(None, "round", "brick", None, None, None, None)
    return jax.shard_map(
        on_device, mesh=mesh, in_specs=in_specs, out_specs=out_specs, check_vma=False
    )
```

time: 158 us -> 58.1 us (0.37)
  blocking collectives: 61.2 us -> 0 us
  local copies, waits for them, and re-layouts: 42.4 us -> 1.58 us
  Pallas kernels: 0 us -> 26.9 us
  matrix products: 23.9 us -> 0 us
  other arithmetic: 17.3 us -> 0.7 us
  starting transfers between devices: 7.6 us -> 20.4 us
  waiting for transfers between devices: 4.18 us -> 7.91 us
    psum x1 -> x0, blocking collectives: 61.2 us -> none  [on_device(): totals = lax.psum(stats, ('round', 'brick'))]
    pallas_call x0 -> x7, Pallas kernels: none -> 26.9 us  [the longest x5 20.6 us: filtered(): pl.pallas_call(functools.partial(filter_kernel, picks, edge, sums is None...]
    dot_general x7 -> x0, matrix products: 23.9 us -> none  [the longest x1 5.29 us: spot_filter(): jnp.einsum('...zyx,wz->...wyx', mixed_y + bent_y, gauss_z, precision=high)]
    gather x2 -> x0, local copies, waits for them, and re-layouts: 21.2 us -> none  [one_brick(): lax.dynamic_slice_in_dim(padded, start, width + 1, 3).astype(jnp.float32)]
    concatenate x2 -> x0, local copies, waits for them, and re-layouts: 20.7 us -> none  [with_halo(): jnp.concatenate([lax.ppermute(tail, axis, [(i, (i + 1) % count) for i in...]
    ppermute x2 -> x11, starting transfers between devices: 3.7 us -> 20.4 us  [the longest x4 10.9 us: on_device(): lax.ppermute(stat, 'brick', [(i, i ^ step) for i in range(count)])]
    convert_element_type x6 -> x0, other arithmetic: 11.4 us -> none  [the longest x1 5.33 us: on_device(): normed = (ratio / jnp.sqrt(energy + 1.0)).astype(jnp.bfloat16)]
    all_to_all x1 -> x0, starting transfers between devices: 3.9 us -> none  [on_device(): lax.all_to_all(filtered[None], 'round', split_axis=1, concat_axis=0, tile...]
  transfers between devices with their start and end apart: 3 -> 11, of which waited for: 1 -> 5; matrix products, arithmetic and copies ran while one was open for 1% -> 1% of each run, Pallas kernels for 0% -> 36%
where the time goes in v1:
time: 58.1 us; the launch traced here: 57.6 us
  Pallas kernels  26.9 us (46%)
  starting transfers between devices  20.4 us (35%)
  waiting for transfers between devices  7.91 us (14%)
  local copies, waits for them, and re-layouts  1.58 us (3%)
  other arithmetic  0.7 us (1%)
    pallas_call x5, Pallas kernels, filtered(): pl.pallas_call(functools.partial(filter_kernel, picks, edge, sums is None...  20.6 us
    ppermute x4, starting transfers between devices, on_device(): lax.ppermute(stat, 'brick', [(i, i ^ step) for i in range(count)])  10.9 us
    ppermute x4, waiting for transfers between devices, on_device(): lax.ppermute(stat, 'brick', [(i, i ^ step) for i in range(count)])  5.79 us
    ppermute x4, starting transfers between devices, on_device(): lax.ppermute(part, 'round', [(i, (i + d) % rounds) for i in range(rounds)])  4.41 us
    pallas_call x1, Pallas kernels, on_device(): pl.pallas_call(functools.partial(norm_kernel, rounds, places), in_specs=[...  3.87 us
    pallas_call x1, Pallas kernels, on_device(): pl.pallas_call(pack_kernel, in_specs=[SMEM, VMEM], out_specs=[VMEM, VMEM]...  2.4 us
    ppermute x1, starting transfers between devices, on_device(): before = lax.ppermute(tail, 'brick', [(i, i + 1) for i in range(ends)])  2.39 us
    ppermute x1, waiting for transfers between devices, on_device(): lax.ppermute(stat, 'round', [(i, (i + d) % rounds) for i in range(rounds)])  2.11 us
  transfers between devices with their start and end apart: 11, of which 5 were waited for; matrix products, arithmetic and copies ran while one was open for 1% of the time, Pallas kernels for 36%

profile of v1, /device:TPU:0, one launch (start us, length us, event | category | flops | bytes accessed | tf_op | source)
XLA Modules:
  0.0 57.6 jit_solution(9490595048606958051)
XLA Ops:
  0.0 2.4 %pack.1 = (bf16[256,128]{1,0:T(8,128)(2,1)}, bf16[256,128]{1,0:T(8,128)(2,1)}) custom-call(s32[128]{0:T(128)} %refs_2_.9, bf16[8,4,256,128]{3,2,1,0:T(8,128)(2,1)} %bitcast.5), custom_call_target="tpu_custom_call" | custom-call | tf_op jit(solution)/shard_map/pack/pallas_call | solution.py:194
  2.4 2.4 %collective-permute-start = (bf16[256,128]{1,0:T(8,128)(2,1)}, bf16[256,128]{1,0:T(8,128)(2,1)S(1)}, u32[]{:S(2)}, u32[]{:S(2)}) collective-permute-start(bf16[256,128]{1,0:T(8,128)(2,1)} %get-tuple-element.17), channel_id=1, source_target_pairs={{0,1},{1,2},{2,3},{3,4},{4,5},{5,6},{6,7},{7,8},{8,9},{9,10},{10,1... | collective-permute-start | bytes 196616 | tf_op jit(solution)/shard_map/ppermute | solution.py:202
  4.8 1.3 %collective-permute-start.1 = (bf16[256,128]{1,0:T(8,128)(2,1)}, bf16[256,128]{1,0:T(8,128)(2,1)S(1)}, u32[]{:S(2)}, u32[]{:S(2)}) collective-permute-start(bf16[256,128]{1,0:T(8,128)(2,1)} %get-tuple-element.18), channel_id=1, source_target_pairs={{1,0},{2,1},{3,2},{4,3},{5,4},{6,5},{7,6},{8,7},{9,8},{10,9},{11,1... | collective-permute-start | bytes 196616 | tf_op jit(solution)/shard_map/ppermute | solution.py:203
  6.1 3.5 %filter1.4 = (bf16[1,4,256,128]{3,2,1,0:T(8,128)(2,1)}, f32[4,8,128]{2,1,0:T(8,128)}) custom-call(s32[1,8]{1,0:T(1,128)} %refs_0_.9, f32[1,8]{1,0:T(1,128)} %refs_1_.9, s32[128]{0:T(128)} %refs_2_.9, bf16[8,4,256,128]{3,2,1,0:T(8,128)(2,1)} %bitcast.6, bf16[2,512,256]{2,1,0:T(8,128)(2,1)} %constant.4.clone.refs_4_, f32[2,256,128]{2,1,0:T(8,128)} %constant.5.clone.refs_5_), custom_call_target="tpu_custom_call" | custom-call | tf_op jit(solution)/shard_map/filter1/pallas_call | solution.py:227
  9.6 3.6 %filter1.5 = (bf16[1,4,256,128]{3,2,1,0:T(8,128)(2,1)}, f32[4,8,128]{2,1,0:T(8,128)}) custom-call(s32[1,8]{1,0:T(1,128)} %refs_0_.9, f32[1,8]{1,0:T(1,128)} %refs_1_.9, s32[128]{0:T(128)} %refs_2_.9, bf16[8,4,256,128]{3,2,1,0:T(8,128)(2,1)} %bitcast.7, bf16[2,512,256]{2,1,0:T(8,128)(2,1)} %constant.4.clone.refs_4_, f32[2,256,128]{2,1,0:T(8,128)} %constant.5.clone.refs_5_, ...), custom_call_target="tpu_custom_call" | custom-call | tf_op jit(solution)/shard_map/filter1/pallas_call | solution.py:227
  13.2 0.0 copy-start.9
  13.2 0.0 copy-start.8
  13.2 3.6 %filter1.6 = (bf16[1,4,256,128]{3,2,1,0:T(8,128)(2,1)}, f32[4,8,128]{2,1,0:T(8,128)}) custom-call(s32[1,8]{1,0:T(1,128)} %refs_0_.9, f32[1,8]{1,0:T(1,128)} %refs_1_.9, s32[128]{0:T(128)} %refs_2_.9, bf16[8,4,256,128]{3,2,1,0:T(8,128)(2,1)} %bitcast.8, bf16[2,512,256]{2,1,0:T(8,128)(2,1)} %constant.4.clone.refs_4_, f32[2,256,128]{2,1,0:T(8,128)} %constant.5.clone.refs_5_, ...), custom_call_target="tpu_custom_call" | custom-call | tf_op jit(solution)/shard_map/filter1/pallas_call | solution.py:227
  16.8 2.3 %collective-permute-start.9 = (bf16[1,4,256,128]{3,2,1,0:T(8,128)(2,1)}, bf16[1,4,256,128]{3,2,1,0:T(8,128)(2,1)S(1)}, u32[]{:S(2)}, u32[]{:S(2)}) collective-permute-start(bf16[1,4,256,128]{3,2,1,0:T(8,128)(2,1)} %get-tuple-element.27), channel_id=1, source_target_pairs={{0,16},{16,0},{1,17},{17,1},{2,18},{18,2},{3,19},{19,3},{4,20},{20... | collective-permute-start | bytes 786440 | tf_op jit(solution)/shard_map/ppermute | solution.py:242
  19.1 0.0 copy-done.9
  19.1 0.1 collective-permute-start.8
  19.2 0.0 copy-done.8
  19.2 2.0 %collective-permute-start.7 = (bf16[1,4,256,128]{3,2,1,0:T(8,128)(2,1)S(1)}, bf16[1,4,256,128]{3,2,1,0:T(8,128)(2,1)S(1)}, u32[]{:S(2)}, u32[]{:S(2)}) collective-permute-start(bf16[1,4,256,128]{3,2,1,0:T(8,128)(2,1)S(1)} %copy-done.8), channel_id=1, source_target_pairs={{0,16},{16,0},{1,17},{17,1},{2,18},{18,2},{3,19},{19,3},{4,20},{20... | collective-permute-start | bytes 786440 | tf_op jit(solution)/shard_map/ppermute | solution.py:242
  21.1 0.0 collective-permute-done.refs_6_
  21.1 0.0 copy-start.4
  21.1 0.0 collective-permute-done.1.refs_7_
  21.1 0.0 copy-start.5
  21.1 0.6 %copy-done.4 = bf16[256,128]{1,0:T(8,128)(2,1)} copy-done((bf16[256,128]{1,0:T(8,128)(2,1)}, bf16[256,128]{1,0:T(8,128)(2,1)S(1)}, u32[]{:S(2)}) %copy-start.4) | copy-done | bytes 65560
  21.7 0.0 copy-done.5
  21.8 3.7 %filter1.7 = (bf16[1,4,256,128]{3,2,1,0:T(8,128)(2,1)}, f32[4,8,128]{2,1,0:T(8,128)}) custom-call(s32[1,8]{1,0:T(1,128)} %refs_0_.9, f32[1,8]{1,0:T(1,128)} %refs_1_.9, s32[128]{0:T(128)} %refs_2_.9, bf16[8,4,256,128]{3,2,1,0:T(8,128)(2,1)} %bitcast.9, bf16[2,512,256]{2,1,0:T(8,128)(2,1)} %constant.4.clone.refs_4_, f32[2,256,128]{2,1,0:T(8,128)} %constant.5.clone.refs_5_, ...), custom_call_target="tpu_custom_call" | custom-call | tf_op jit(solution)/shard_map/filter1/pallas_call | solution.py:227
  25.4 0.1 collective-permute-start.10
  25.5 6.3 %filter4.1 = (bf16[4,4,256,128]{3,2,1,0:T(8,128)(2,1)}, f32[8,128]{1,0:T(8,128)}) custom-call(s32[1,8]{1,0:T(1,128)} %refs_0_.9, f32[1,8]{1,0:T(1,128)} %refs_1_.9, s32[128]{0:T(128)} %refs_2_.9, bf16[8,4,256,128]{3,2,1,0:T(8,128)(2,1)} %bitcast.10, bf16[2,512,256]{2,1,0:T(8,128)(2,1)} %constant.4.clone.refs_4_, f32[2,256,128]{2,1,0:T(8,128)} %constant.5.clone.refs_5_, ...), custom_call_target="tpu_custom_call" | custom-call | tf_op jit(solution)/shard_map/filter4/pallas_call | solution.py:227
  31.8 1.8 %collective-permute-start.2 = (f32[8,128]{1,0:T(8,128)}, f32[8,128]{1,0:T(8,128)S(1)}, u32[]{:S(2)}, u32[]{:S(2)}) collective-permute-start(f32[8,128]{1,0:T(8,128)} %get-tuple-element.24), channel_id=1, source_target_pairs={{0,1},{1,0},{2,3},{3,2},{4,5},{5,4},{6,7},{7,6},{8,9},{9,8},{10,11... | collective-permute-start | bytes 12296 | tf_op jit(solution)/shard_map/ppermute | solution.py:247
  33.6 1.0 %collective-permute-done.2 = f32[8,128]{1,0:T(8,128)S(1)} collective-permute-done((f32[8,128]{1,0:T(8,128)}, f32[8,128]{1,0:T(8,128)S(1)}, u32[]{:S(2)}, u32[]{:S(2)}) %collective-permute-start.2) | collective-permute-done | bytes 4128 | tf_op jit(solution)/shard_map/ppermute | solution.py:247
  34.6 0.7 %add.12 = f32[8,128]{1,0:T(8,128)S(1)} add(f32[8,128]{1,0:T(8,128)} %get-tuple-element.24, f32[8,128]{1,0:T(8,128)S(1)} %collective-permute-done.2) | non-fusion elementwise | flops 1024 | bytes 12288 | tf_op jit(solution)/shard_map/add | solution.py:247
  35.3 3.1 %collective-permute-start.3 = (f32[8,128]{1,0:T(8,128)S(1)}, f32[8,128]{1,0:T(8,128)S(1)}, u32[]{:S(2)}, u32[]{:S(2)}) collective-permute-start(f32[8,128]{1,0:T(8,128)S(1)} %add.12), channel_id=1, source_target_pairs={{0,2},{1,3},{2,0},{3,1},{4,6},{5,7},{6,4},{7,5},{8,10},{9,11},{10,... | collective-permute-start | bytes 12296 | tf_op jit(solution)/shard_map/ppermute | solution.py:247
  38.4 1.6 %collective-permute-done.3 = f32[8,128]{1,0:T(8,128)S(1)} collective-permute-done((f32[8,128]{1,0:T(8,128)S(1)}, f32[8,128]{1,0:T(8,128)S(1)}, u32[]{:S(2)}, u32[]{:S(2)}) %collective-permute-start.3) | collective-permute-done | bytes 4128 | tf_op jit(solution)/shard_map/ppermute | solution.py:247
  40.0 3.0 %collective-permute-start.4 = (f32[8,128]{1,0:T(8,128)S(1)}, f32[8,128]{1,0:T(8,128)S(1)}, u32[]{:S(2)}, u32[]{:S(2)}) collective-permute-start(f32[8,128]{1,0:T(8,128)S(1)} %add.13), channel_id=1, source_target_pairs={{0,4},{1,5},{2,6},{3,7},{4,0},{5,1},{6,2},{7,3},{8,12},{9,13},{10,... | collective-permute-start | bytes 12296 | tf_op jit(solution)/shard_map/ppermute | solution.py:247
  42.9 1.6 %collective-permute-done.4 = f32[8,128]{1,0:T(8,128)S(1)} collective-permute-done((f32[8,128]{1,0:T(8,128)S(1)}, f32[8,128]{1,0:T(8,128)S(1)}, u32[]{:S(2)}, u32[]{:S(2)}) %collective-permute-start.4) | collective-permute-done | bytes 4128 | tf_op jit(solution)/shard_map/ppermute | solution.py:247
  44.5 3.0 %collective-permute-start.5 = (f32[8,128]{1,0:T(8,128)S(1)}, f32[8,128]{1,0:T(8,128)S(1)}, u32[]{:S(2)}, u32[]{:S(2)}) collective-permute-start(f32[8,128]{1,0:T(8,128)S(1)} %add.14), channel_id=1, source_target_pairs={{0,8},{1,9},{2,10},{3,11},{4,12},{5,13},{6,14},{7,15},{8,0},{9,1},... | collective-permute-start | bytes 12296 | tf_op jit(solution)/shard_map/ppermute | solution.py:247
  47.6 1.6 %collective-permute-done.5 = f32[8,128]{1,0:T(8,128)S(1)} collective-permute-done((f32[8,128]{1,0:T(8,128)S(1)}, f32[8,128]{1,0:T(8,128)S(1)}, u32[]{:S(2)}, u32[]{:S(2)}) %collective-permute-start.5) | collective-permute-done | bytes 4128 | tf_op jit(solution)/shard_map/ppermute | solution.py:247
  49.1 0.0 copy-start.6
  49.1 1.5 %collective-permute-start.6 = (f32[8,128]{1,0:T(8,128)S(1)}, f32[8,128]{1,0:T(8,128)S(1)}, u32[]{:S(2)}, u32[]{:S(2)}) collective-permute-start(f32[8,128]{1,0:T(8,128)S(1)} %add.15.refs_2_), channel_id=1, source_target_pairs={{0,16},{16,0},{1,17},{17,1},{2,18},{18,2},{3,19},{19,3},{4,20},{20... | collective-permute-start | bytes 12296 | tf_op jit(solution)/shard_map/ppermute | solution.py:251
  50.6 2.1 %collective-permute-done.6.refs_3_ = f32[8,128]{1,0:T(8,128)S(1)} collective-permute-done((f32[8,128]{1,0:T(8,128)S(1)}, f32[8,128]{1,0:T(8,128)S(1)}, u32[]{:S(2)}, u32[]{:S(2)}) %collective-permute-start.6) | collective-permute-done | bytes 4128 | tf_op jit(solution)/shard_map/ppermute | solution.py:251
  52.8 0.0 copy-start.7
  52.8 0.0 collective-permute-done.9.refs_6_
  52.8 0.0 copy-start
  52.8 0.0 collective-permute-done.8.refs_5_
  52.8 0.0 copy-start.1
  52.8 0.0 collective-permute-done.7.refs_4_
  52.8 0.0 copy-start.2
  52.8 0.0 collective-permute-done.10.refs_7_
  52.8 0.0 copy-start.3
  52.8 0.0 copy-done.6
  52.8 0.5 copy-done.7
  53.3 0.1 copy-done
  53.5 0.1 copy-done.1
  53.6 0.1 copy-done.2
  53.7 0.1 copy-done.3
  53.8 3.9 %norm.1 = bf16[2,1,4,4,256,128]{5,4,3,2,1,0:T(8,128)(2,1)} custom-call(s32[1,128]{1,0:T(1,128)} %bitcast.11, bf16[4,4,256,128]{3,2,1,0:T(8,128)(2,1)} %get-tuple-element.23.refs_1_, f32[8,128]{1,0:T(8,128)} %copy-done.6, f32[8,128]{1,0:T(8,128)} %copy-done.7, bf16[1,4,256,128]{3,2,1,0:T(8,128)(2,1)} %copy-done.2, bf16[1,4,256,128]{3,2,1,0:T(8,128)(2,1)} %copy-done.1, ...), custom_call_target="tpu_custom_call" | custom-call | tf_op jit(solution)/shard_map/norm/pallas_call | solution.py:253
  (3 shorter events, 0.0 us)
Async XLA Ops:
  2.4 18.7 %collective-permute-start = (bf16[256,128]{1,0:T(8,128)(2,1)}, bf16[256,128]{1,0:T(8,128)(2,1)S(1)}, u32[]{:S(2)}, u32[]{:S(2)}) collective-permute-start(bf16[256,128]{1,0:T(8,128)(2,1)} %get-tuple-element.17), channel_id=1, source_target_pairs={{0,1},{1,2},{2,3},{3,4},{4,5},{5,6},{6,7},{7,8},{8,9},{9,10},{10,1... | collective-permute-start | bytes 196616 | tf_op jit(solution)/shard_map/ppermute | solution.py:202
  4.8 16.3 %collective-permute-start.1 = (bf16[256,128]{1,0:T(8,128)(2,1)}, bf16[256,128]{1,0:T(8,128)(2,1)S(1)}, u32[]{:S(2)}, u32[]{:S(2)}) collective-permute-start(bf16[256,128]{1,0:T(8,128)(2,1)} %get-tuple-element.18), channel_id=1, source_target_pairs={{1,0},{2,1},{3,2},{4,3},{5,4},{6,5},{7,6},{8,7},{9,8},{10,9},{11,1... | collective-permute-start | bytes 196616 | tf_op jit(solution)/shard_map/ppermute | solution.py:203
  13.2 5.9 %copy-start.9 = (bf16[1,4,256,128]{3,2,1,0:T(8,128)(2,1)S(1)}, bf16[1,4,256,128]{3,2,1,0:T(8,128)(2,1)}, u32[]{:S(2)}) copy-start(bf16[1,4,256,128]{3,2,1,0:T(8,128)(2,1)} %get-tuple-element.26) | copy-start | bytes 786436
  13.2 6.0 %copy-start.8 = (bf16[1,4,256,128]{3,2,1,0:T(8,128)(2,1)S(1)}, bf16[1,4,256,128]{3,2,1,0:T(8,128)(2,1)}, u32[]{:S(2)}) copy-start(bf16[1,4,256,128]{3,2,1,0:T(8,128)(2,1)} %get-tuple-element.25) | copy-start | bytes 786436
  16.8 36.0 %collective-permute-start.9 = (bf16[1,4,256,128]{3,2,1,0:T(8,128)(2,1)}, bf16[1,4,256,128]{3,2,1,0:T(8,128)(2,1)S(1)}, u32[]{:S(2)}, u32[]{:S(2)}) collective-permute-start(bf16[1,4,256,128]{3,2,1,0:T(8,128)(2,1)} %get-tuple-element.27), channel_id=1, source_target_pairs={{0,16},{16,0},{1,17},{17,1},{2,18},{18,2},{3,19},{19,3},{4,20},{20... | collective-permute-start | bytes 786440 | tf_op jit(solution)/shard_map/ppermute | solution.py:242
  19.1 33.7 %collective-permute-start.8 = (bf16[1,4,256,128]{3,2,1,0:T(8,128)(2,1)S(1)}, bf16[1,4,256,128]{3,2,1,0:T(8,128)(2,1)S(1)}, u32[]{:S(2)}, u32[]{:S(2)}) collective-permute-start(bf16[1,4,256,128]{3,2,1,0:T(8,128)(2,1)S(1)} %copy-done.9), channel_id=1, source_target_pairs={{0,16},{16,0},{1,17},{17,1},{2,18},{18,2},{3,19},{19,3},{4,20},{20... | collective-permute-start | bytes 786440 | tf_op jit(solution)/shard_map/ppermute | solution.py:242
  19.2 33.6 %collective-permute-start.7 = (bf16[1,4,256,128]{3,2,1,0:T(8,128)(2,1)S(1)}, bf16[1,4,256,128]{3,2,1,0:T(8,128)(2,1)S(1)}, u32[]{:S(2)}, u32[]{:S(2)}) collective-permute-start(bf16[1,4,256,128]{3,2,1,0:T(8,128)(2,1)S(1)} %copy-done.8), channel_id=1, source_target_pairs={{0,16},{16,0},{1,17},{17,1},{2,18},{18,2},{3,19},{19,3},{4,20},{20... | collective-permute-start | bytes 786440 | tf_op jit(solution)/shard_map/ppermute | solution.py:242
  21.1 0.6 %copy-start.4 = (bf16[256,128]{1,0:T(8,128)(2,1)}, bf16[256,128]{1,0:T(8,128)(2,1)S(1)}, u32[]{:S(2)}) copy-start(bf16[256,128]{1,0:T(8,128)(2,1)S(1)} %collective-permute-done.refs_6_) | copy-start | bytes 196612
  21.1 0.6 %copy-start.5 = (bf16[256,128]{1,0:T(8,128)(2,1)}, bf16[256,128]{1,0:T(8,128)(2,1)S(1)}, u32[]{:S(2)}) copy-start(bf16[256,128]{1,0:T(8,128)(2,1)S(1)} %collective-permute-done.1.refs_7_) | copy-start | bytes 196612
  25.4 27.4 %collective-permute-start.10 = (bf16[1,4,256,128]{3,2,1,0:T(8,128)(2,1)}, bf16[1,4,256,128]{3,2,1,0:T(8,128)(2,1)S(1)}, u32[]{:S(2)}, u32[]{:S(2)}) collective-permute-start(bf16[1,4,256,128]{3,2,1,0:T(8,128)(2,1)} %get-tuple-element.28), channel_id=1, source_target_pairs={{0,16},{16,0},{1,17},{17,1},{2,18},{18,2},{3,19},{19,3},{4,20},{20... | collective-permute-start | bytes 786440 | tf_op jit(solution)/shard_map/ppermute | solution.py:242
  31.8 2.8 %collective-permute-start.2 = (f32[8,128]{1,0:T(8,128)}, f32[8,128]{1,0:T(8,128)S(1)}, u32[]{:S(2)}, u32[]{:S(2)}) collective-permute-start(f32[8,128]{1,0:T(8,128)} %get-tuple-element.24), channel_id=1, source_target_pairs={{0,1},{1,0},{2,3},{3,2},{4,5},{5,4},{6,7},{7,6},{8,9},{9,8},{10,11... | collective-permute-start | bytes 12296 | tf_op jit(solution)/shard_map/ppermute | solution.py:247
  35.3 4.7 %collective-permute-start.3 = (f32[8,128]{1,0:T(8,128)S(1)}, f32[8,128]{1,0:T(8,128)S(1)}, u32[]{:S(2)}, u32[]{:S(2)}) collective-permute-start(f32[8,128]{1,0:T(8,128)S(1)} %add.12), channel_id=1, source_target_pairs={{0,2},{1,3},{2,0},{3,1},{4,6},{5,7},{6,4},{7,5},{8,10},{9,11},{10,... | collective-permute-start | bytes 12296 | tf_op jit(solution)/shard_map/ppermute | solution.py:247
  40.0 4.6 %collective-permute-start.4 = (f32[8,128]{1,0:T(8,128)S(1)}, f32[8,128]{1,0:T(8,128)S(1)}, u32[]{:S(2)}, u32[]{:S(2)}) collective-permute-start(f32[8,128]{1,0:T(8,128)S(1)} %add.13), channel_id=1, source_target_pairs={{0,4},{1,5},{2,6},{3,7},{4,0},{5,1},{6,2},{7,3},{8,12},{9,13},{10,... | collective-permute-start | bytes 12296 | tf_op jit(solution)/shard_map/ppermute | solution.py:247
  44.5 4.6 %collective-permute-start.5 = (f32[8,128]{1,0:T(8,128)S(1)}, f32[8,128]{1,0:T(8,128)S(1)}, u32[]{:S(2)}, u32[]{:S(2)}) collective-permute-start(f32[8,128]{1,0:T(8,128)S(1)} %add.14), channel_id=1, source_target_pairs={{0,8},{1,9},{2,10},{3,11},{4,12},{5,13},{6,14},{7,15},{8,0},{9,1},... | collective-permute-start | bytes 12296 | tf_op jit(solution)/shard_map/ppermute | solution.py:247
  49.1 3.7 %copy-start.6 = (f32[8,128]{1,0:T(8,128)}, f32[8,128]{1,0:T(8,128)S(1)}, u32[]{:S(2)}) copy-start(f32[8,128]{1,0:T(8,128)S(1)} %add.15.refs_2_) | copy-start | bytes 12292
  49.1 3.6 %collective-permute-start.6 = (f32[8,128]{1,0:T(8,128)S(1)}, f32[8,128]{1,0:T(8,128)S(1)}, u32[]{:S(2)}, u32[]{:S(2)}) collective-permute-start(f32[8,128]{1,0:T(8,128)S(1)} %add.15.refs_2_), channel_id=1, source_target_pairs={{0,16},{16,0},{1,17},{17,1},{2,18},{18,2},{3,19},{19,3},{4,20},{20... | collective-permute-start | bytes 12296 | tf_op jit(solution)/shard_map/ppermute | solution.py:251
  52.8 0.6 %copy-start.7 = (f32[8,128]{1,0:T(8,128)}, f32[8,128]{1,0:T(8,128)S(1)}, u32[]{:S(2)}) copy-start(f32[8,128]{1,0:T(8,128)S(1)} %collective-permute-done.6.refs_3_) | copy-start | bytes 12292
  52.8 0.7 %copy-start = (bf16[1,4,256,128]{3,2,1,0:T(8,128)(2,1)}, bf16[1,4,256,128]{3,2,1,0:T(8,128)(2,1)S(1)}, u32[]{:S(2)}) copy-start(bf16[1,4,256,128]{3,2,1,0:T(8,128)(2,1)S(1)} %collective-permute-done.9.refs_6_) | copy-start | bytes 786436
  52.8 0.8 %copy-start.1 = (bf16[1,4,256,128]{3,2,1,0:T(8,128)(2,1)}, bf16[1,4,256,128]{3,2,1,0:T(8,128)(2,1)S(1)}, u32[]{:S(2)}) copy-start(bf16[1,4,256,128]{3,2,1,0:T(8,128)(2,1)S(1)} %collective-permute-done.8.refs_5_) | copy-start | bytes 786436
  52.8 0.9 %copy-start.2 = (bf16[1,4,256,128]{3,2,1,0:T(8,128)(2,1)}, bf16[1,4,256,128]{3,2,1,0:T(8,128)(2,1)S(1)}, u32[]{:S(2)}) copy-start(bf16[1,4,256,128]{3,2,1,0:T(8,128)(2,1)S(1)} %collective-permute-done.7.refs_4_) | copy-start | bytes 786436
  52.8 0.9 %copy-start.3 = (bf16[1,4,256,128]{3,2,1,0:T(8,128)(2,1)}, bf16[1,4,256,128]{3,2,1,0:T(8,128)(2,1)S(1)}, u32[]{:S(2)}) copy-start(bf16[1,4,256,128]{3,2,1,0:T(8,128)(2,1)S(1)} %collective-permute-done.10.refs_7_) | copy-start | bytes 786436

commit v2 on v1

v2 whole, which is shorter than its diff:
```python
import functools

import jax
import jax.numpy as jnp
import numpy as np
from jax import lax
from jax.experimental import pallas as pl
from jax.experimental.pallas import tpu as pltpu
from jax.sharding import PartitionSpec as P

sigma_spot = 1.5


BF = jnp.bfloat16
F32 = jnp.float32
VMEM = pl.BlockSpec(memory_space=pltpu.VMEM)
SMEM = pl.BlockSpec(memory_space=pltpu.SMEM)
HBM = pl.BlockSpec(memory_space=pltpu.HBM)
PARAMS = pltpu.CompilerParams(vmem_limit_bytes=24 * 2**20)


def kernel_tables(count):
    index = np.arange(count, dtype=np.float64)
    offset = index[:, None] - index[None, :]
    smooth = np.exp(-offset * offset / (2.0 * sigma_spot * sigma_spot)) / (
        2.5066282746310002 * sigma_spot
    )
    smooth = np.where(np.abs(offset) < 4.0 * sigma_spot, smooth, 0.0)
    curve = (offset * offset / sigma_spot**4 - 1.0 / sigma_spot**2) * smooth
    return smooth, curve


def plane_tables(depth, height):
    gauss_z, curve_z = kernel_tables(depth)
    gauss_y, curve_y = kernel_tables(height)
    factor = -(sigma_spot * sigma_spot)
    with_bent = np.kron(gauss_z, gauss_y)
    with_smooth = np.kron(gauss_z, curve_y) + np.kron(curve_z, gauss_y)
    table = (factor * np.concatenate([with_bent, with_smooth], axis=0)).astype(np.float32)
    high = table.astype(BF)
    low = (table - high.astype(np.float32)).astype(BF)
    return np.concatenate([high, low], axis=0)


def line_tables(width):
    gauss_x, curve_x = kernel_tables(width)
    return np.stack([np.tile(t.T, (2, 1)) for t in (curve_x, gauss_x)]).astype(np.float32)


def lanes_of(shape):
    return lax.broadcasted_iota(jnp.int32, shape, len(shape) - 1)


def pack_kernel(valid_ref, img_ref, tail_ref, head_ref):
    bricks, channels, plane, width = img_ref.shape
    slot = width // channels
    first = lax.axis_index("brick") * bricks
    lane = lanes_of((plane, width))

    def pack(brick, at):
        row = jnp.zeros((plane, width), F32)
        for c in range(channels):
            data = img_ref[brick, c].astype(F32)
            amount = (c * slot - at) % width
            moved = pltpu.roll(data, amount, 1) if amount else data
            row = jnp.where(lane // slot == c, moved, row)
        return (row * valid_ref[first + brick].astype(F32)).astype(BF)

    tail_ref[...] = pack(bricks - 1, width - slot)
    head_ref[...] = pack(0, 0)


class Filter:
    def __init__(self, shift_ref, frac_ref, valid_ref, img_ref, plane_ref, line_ref, halo=None):
        self.shift, self.frac, self.valid = shift_ref, frac_ref, valid_ref
        self.img, self.plane, self.line, self.halo = img_ref, plane_ref, line_ref, halo

    def __call__(self, b, put, totals):
        bricks, channels, plane, width = self.img.shape
        slot = width // channels
        first = lax.axis_index("brick") * bricks
        lane = lanes_of((1, width))
        s = self.shift[0, b]
        f = self.frac[0, b]
        right = s >= 0
        nb = jnp.where(right, b - 1, b + 1)
        nb_in = jnp.clip(nb, 0, bricks - 1)
        own_valid = self.valid[first + b].astype(F32)
        nb_valid = self.valid[first + nb_in].astype(F32)
        if self.halo:
            nb_valid = jnp.where(nb == nb_in, nb_valid, 1.0)
        low0, high0 = jnp.where(right, 0, -s), jnp.where(right, width - s, width)
        low1, high1 = jnp.where(right, 0, -s - 1), jnp.where(right, width - s - 1, width)
        own0 = (lane >= low0) & (lane < high0)
        own1 = (lane >= low1) & (lane < high1)
        gain0 = (1.0 - f) * jnp.where(own0, own_valid, nb_valid)
        gain1 = f * jnp.where(own1, own_valid, nb_valid)
        own0, own1 = (jnp.broadcast_to(m, (plane, width)) for m in (own0, own1))
        parts = []
        for c in range(channels):
            own = self.img[b, c].astype(F32)
            other = self.img[nb_in, c].astype(F32)
            if self.halo:
                tail_ref, head_ref = self.halo
                before = pltpu.roll(tail_ref[...].astype(F32), (width - slot - c * slot) % width, 1)
                after = head_ref[...].astype(F32)
                if c:
                    after = pltpu.roll(after, (width - c * slot) % width, 1)
                other = jnp.where(nb < 0, before, jnp.where(nb >= bricks, after, other))
            here = jnp.where(own0, own, other) * gain0
            there = jnp.where(own1, own, other) * gain1
            parts.append((here + pltpu.roll(there, 1, 1)).astype(BF))
        field = jnp.concatenate(parts, axis=1)
        dot = functools.partial(jnp.dot, preferred_element_type=F32)
        half = 2 * plane
        mixed = dot(self.plane[:half], field) + dot(self.plane[half:], field)
        turn = jnp.where(s < 0, s + width, s)
        line = jnp.concatenate([self.line[k, pl.ds(turn, width), :] for k in range(2)], axis=0)
        line_high = line.astype(BF)
        line_low = (line - line_high.astype(F32)).astype(BF)
        lines = jnp.concatenate([line_high, line_low], axis=1)
        added = []
        for c in range(channels):
            wide = jnp.concatenate(
                [mixed[k * plane : (k + 1) * plane, c * width : (c + 1) * width] for k in range(2)],
                axis=1,
            )
            both = dot(wide.astype(BF), lines)
            result = (both[:, :width] + both[:, width:]).astype(BF)
            put(c, result)
            size = jnp.abs(result.astype(F32)).reshape(plane // 8, 8, width)
            added.append(totals[c] + jnp.sum(size, axis=0) * own_valid)
        return added


def no_totals(channels, width):
    return [jnp.zeros((8, width), F32) for _ in range(channels)]


def put_in(ref, n):
    def put(c, value):
        ref[n, c] = value

    return put


def load_kernel(picks, shift_ref, frac_ref, valid_ref, img_ref, plane_ref, line_ref, *refs):
    *part_refs, stat_ref, img_out, plane_out, line_out, brick_sem, table_sem = refs
    bricks, channels, _, width = img_ref.shape
    rank = lax.axis_index("round")
    copies = {}

    def fetch(b):
        return pltpu.make_async_copy(img_ref.at[b], img_out.at[b], brick_sem.at[b])

    tables = [
        pltpu.make_async_copy(plane_ref, plane_out, table_sem.at[0]),
        pltpu.make_async_copy(line_ref, line_out, table_sem.at[1]),
    ]
    if picks:
        base = picks[0](rank) - 1
    else:
        base = 0
    order = [lax.rem(base + n, bricks) for n in range(bricks)]
    for n, b in enumerate(order):
        copies[n] = fetch(b)
        copies[n].start()
        if n == 2:
            for table in tables:
                table.start()
    waited = 0
    totals = no_totals(channels, width)
    if picks:
        for waited in range(3):
            copies[waited].wait()
        for table in tables:
            table.wait()
        one = Filter(shift_ref, frac_ref, valid_ref, img_out, plane_out, line_out)
        totals = one(picks[0](rank), put_in(part_refs[0], 0), totals)
        waited = 3
    for n in range(waited, bricks):
        copies[n].wait()
    if picks:
        for k, pick in enumerate(picks[1:]):
            totals = one(pick(rank), put_in(part_refs[k + 1], 0), totals)
    else:
        for table in tables:
            table.wait()
    for c in range(channels):
        stat_ref[c] = totals[c]


def filter_kernel(groups, edge, last, shift_ref, frac_ref, valid_ref, img_ref, plane_ref, line_ref, sums_ref, *refs):
    halo = None
    if edge:
        halo, refs = refs[:2], refs[2:]
    *out_refs, stat_ref = refs
    _, channels, _, width = img_ref.shape
    rank = lax.axis_index("round")
    inner = Filter(shift_ref, frac_ref, valid_ref, img_ref, plane_ref, line_ref)
    outer = Filter(shift_ref, frac_ref, valid_ref, img_ref, plane_ref, line_ref, halo)
    totals = [sums_ref[c] for c in range(channels)]
    for picks, out_ref in zip(groups, out_refs, strict=True):
        for n, (pick, on_edge) in enumerate(picks):
            one = outer if on_edge else inner
            totals = one(pick(rank), put_in(out_ref, n), totals)
    if last:
        row = lax.broadcasted_iota(jnp.int32, (8, width), 0)
        packed = jnp.zeros((8, width), F32)
        for c in range(channels):
            packed = jnp.where(row == c, jnp.sum(totals[c]), packed)
        stat_ref[...] = packed
    else:
        for c in range(channels):
            stat_ref[c] = totals[c]


def norm_kernel(rounds, places, *refs):
    valid_ref, own_ref = refs[:2]
    stat_refs = refs[2 : 2 + rounds]
    *chunk_refs, out_ref, buf_ref, sem = refs[2 + rounds :]
    quota, channels, plane, width = own_ref.shape
    rank = lax.axis_index("round")
    count = jnp.maximum(jnp.sum(valid_ref[...]).astype(F32), 1.0)
    inverse = []
    for d in range(rounds):
        scale = stat_refs[d][...] / (count * (plane * width)) + 1e-06
        inverse.append(1.0 / scale)
    copies = []
    for j in range(quota):
        pos = jnp.where(rank == 0, quota - 1 - j, j)
        energy = jnp.zeros((plane, width), F32)

        def ratio(d, c):
            if d == 0:
                data = own_ref[j, c]
            else:
                g, n = places[d, j]
                data = chunk_refs[g][n, c]
            return data.astype(F32) * inverse[d][c : c + 1, :]

        for d in range(rounds):
            for c in range(channels):
                part = ratio(d, c)
                energy = energy + part * part
        factor = lax.rsqrt(energy * (1.0 / (rounds * channels)) + 1.0)
        for d in range(rounds):
            slot = lax.rem(rank + rounds - d, rounds)
            for c in range(channels):
                buf_ref[j, d, c] = (ratio(d, c) * factor).astype(BF)
            copy = pltpu.make_async_copy(buf_ref.at[j, d], out_ref.at[slot, 0, pos], sem.at[j, d])
            copy.start()
            copies.append(copy)
    for copy in copies:
        copy.wait()


def in_vmem(x):
    return pltpu.with_memory_space_constraint(x, pltpu.VMEM)


def in_hbm(x):
    return pltpu.with_memory_space_constraint(x, pltpu.HBM)


def body(image, shifts, fractions, valid):
    _, bricks, channels, depth, height, width = image.shape
    plane = depth * height
    rounds = lax.axis_size("round")
    count = lax.axis_size("brick")
    quota = bricks // rounds
    img = image.reshape(bricks, channels, plane, width)
    plane_table = jnp.asarray(plane_tables(depth, height))
    line_table = jnp.asarray(line_tables(width))

    def out(shape, dtype):
        return pltpu.VMEM(shape, dtype)

    def pick_for(d, j):
        def pick(rank):
            target = lax.rem(rank + d, rounds)
            return target * quota + jnp.where(target == 0, quota - 1 - j, j)

        return pick

    peers = range(1, rounds)
    early = [0] if quota > 1 else []
    inner = list(range(1, quota - 1))
    scalars = [shifts, fractions, valid]
    sum_shape = out((channels, 8, width), F32)

    *parts, sums, img_v, plane_v, line_v = pl.pallas_call(
        functools.partial(load_kernel, [pick_for(d, 0) for d in peers] if early else []),
        in_specs=[SMEM] * 3 + [HBM] * 3,
        out_specs=[VMEM] * ((rounds - 1) * len(early) + 4),
        out_shape=[out((1, channels, plane, width), BF)] * ((rounds - 1) * len(early))
        + [sum_shape, out(img.shape, BF), out(plane_table.shape, BF), out(line_table.shape, F32)],
        scratch_shapes=[pltpu.SemaphoreType.DMA((bricks,)), pltpu.SemaphoreType.DMA((2,))],
        name="load",
        compiler_params=PARAMS,
    )(*[in_hbm(a) for a in (*scalars, img, plane_table, line_table)])

    places = {}
    chunks = []

    def send(parts, js):
        for d, part in zip(peers, parts, strict=True):
            for n, j in enumerate(js):
                places[d, j] = len(chunks), n
            chunks.append(lax.ppermute(part, "round", [(i, (i + d) % rounds) for i in range(rounds)]))

    if early:
        send(parts, early)

    tail, head = pl.pallas_call(
        pack_kernel,
        in_specs=[SMEM, VMEM],
        out_specs=[VMEM, VMEM],
        out_shape=[out((plane, width), BF)] * 2,
        name="pack",
        compiler_params=PARAMS,
    )(valid, in_vmem(img_v))
    ends = count - 1
    before = lax.ppermute(tail, "brick", [(i, i + 1) for i in range(ends)])
    after = lax.ppermute(head, "brick", [(i + 1, i) for i in range(ends)])

    def filtered(groups, edge, last, sums):
        halo = [in_vmem(before), in_vmem(after)] if edge else []
        ins = [in_vmem(a) for a in (img_v, plane_v, line_v, sums)] + halo
        *parts, stat = pl.pallas_call(
            functools.partial(filter_kernel, groups, edge, last),
            in_specs=[SMEM] * 3 + [VMEM] * len(ins),
            out_specs=[VMEM] * (len(groups) + 1),
            out_shape=[out((len(g), channels, plane, width), BF) for g in groups]
            + [out((8, width), F32) if last else sum_shape],
            compiler_params=PARAMS,
        )(*scalars, *ins)
        return parts, stat

    if inner:
        parts, sums = filtered([[(pick_for(d, j), False) for j in inner] for d in peers], False, False, sums)
        send(parts, inner)
    edges = [quota - 1]
    groups = [[(pick_for(d, j), True) for j in edges] for d in peers]
    groups.append([(pick_for(0, j), j == quota - 1) for j in range(quota)])
    (*parts, own), stat = filtered(groups, True, True, sums)
    send(parts, edges)

    step = 1
    while step < count:
        stat = stat + lax.ppermute(stat, "brick", [(i, i ^ step) for i in range(count)])
        step *= 2
    stats = [stat]
    for d in peers:
        stats.append(lax.ppermute(stat, "round", [(i, (i + d) % rounds) for i in range(rounds)]))

    result = pl.pallas_call(
        functools.partial(norm_kernel, rounds, places),
        in_specs=[VMEM] * (2 + rounds + len(chunks)),
        out_specs=HBM,
        out_shape=jax.ShapeDtypeStruct((rounds, 1, quota, channels, plane, width), BF),
        scratch_shapes=[
            pltpu.VMEM((quota, rounds, channels, plane, width), BF),
            pltpu.SemaphoreType.DMA((quota, rounds)),
        ],
        name="norm",
        compiler_params=PARAMS,
    )(valid.reshape(1, -1), *[in_vmem(a) for a in (own, *stats, *chunks)])
    return result.reshape(rounds, 1, quota, channels, depth, height, width)


def solution(mesh):
    in_specs = (
        P("round", "brick", None, None, None, None),
        P("round", "brick"),
        P("round", "brick"),
        P(),
    )
    out_specs = P(None, "round", "brick", None, None, None, None)
    return jax.shard_map(body, mesh=mesh, in_specs=in_specs, out_specs=out_specs, check_vma=False)
```

time: 58.1 us -> 40.5 us (0.70)
  Pallas kernels: 26.9 us -> 11.1 us
  waiting for transfers between devices: 7.91 us -> 11.6 us
  starting transfers between devices: 20.4 us -> 17.5 us
  local copies, waits for them, and re-layouts: 1.58 us -> 0.01 us
  other arithmetic: 0.7 us -> 0.01 us
    pallas_call x7 -> x5, Pallas kernels: 26.9 us -> 11.1 us  [the longest x2 5.41 us: filtered(): pl.pallas_call(functools.partial(filter_kernel, groups, edge, last), in_s...]
    ppermute x11 -> x10, waiting for transfers between devices: 7.91 us -> 11.6 us  [the longest x4 6.37 us: body(): lax.ppermute(stat, 'brick', [(i, i ^ step) for i in range(count)])]
    ppermute x11 -> x10, starting transfers between devices: 20.4 us -> 17.5 us  [the longest x4 9.23 us: body(): lax.ppermute(stat, 'brick', [(i, i ^ step) for i in range(count)])]
    unnamed x20 -> x6, local copies, waits for them, and re-layouts: 1.58 us -> 0.01 us
    add x4, other arithmetic: 0.7 us -> 0.01 us  [body(): stat + lax.ppermute(stat, 'brick', [(i, i ^ step) for i in range(count)])]
  transfers between devices with their start and end apart: 11 -> 10, of which waited for: 5 -> 6; matrix products, arithmetic and copies ran while one was open for 1% -> 0% of each run, Pallas kernels for 36% -> 11%
where the time goes in v2:
time: 40.5 us; the launch traced here: 40.3 us
  starting transfers between devices  17.5 us (43%)
  waiting for transfers between devices  11.6 us (29%)
  Pallas kernels  11.1 us (27%)
    ppermute x4, starting transfers between devices, body(): lax.ppermute(stat, 'brick', [(i, i ^ step) for i in range(count)])  9.23 us
    ppermute x4, waiting for transfers between devices, body(): lax.ppermute(stat, 'brick', [(i, i ^ step) for i in range(count)])  6.37 us
    pallas_call x2, Pallas kernels, filtered(): pl.pallas_call(functools.partial(filter_kernel, groups, edge, last), in_s...  5.41 us
    ppermute x3, starting transfers between devices, send(): lax.ppermute(part, 'round', [(i, (i + d) % rounds) for i in range(rounds)])  4.01 us
    ppermute x1, waiting for transfers between devices, body(): after = lax.ppermute(head, 'brick', [(i + 1, i) for i in range(ends)])  3.07 us
    pallas_call x1, Pallas kernels, body(): pl.pallas_call(functools.partial(load_kernel, [pick_for(d, 0) for d in pe...  3.02 us
    ppermute x1, waiting for transfers between devices, body(): lax.ppermute(stat, 'round', [(i, (i + d) % rounds) for i in range(rounds)])  2.13 us
    pallas_call x1, Pallas kernels, body(): pl.pallas_call(functools.partial(norm_kernel, rounds, places), in_specs=[...  1.99 us
  transfers between devices with their start and end apart: 10, of which 6 were waited for; matrix products, arithmetic and copies ran while one was open for 0% of the time, Pallas kernels for 11%

profile of v2, /device:TPU:0, one launch (start us, length us, event | category | flops | bytes accessed | tf_op | source)
XLA Modules:
  0.0 40.3 jit_solution(5531691042062361855)
XLA Ops:
  0.0 0.0 copy-start
  0.0 0.0 copy-start.2
  0.0 0.0 copy-start.1
  0.0 3.0 %load.1 = (bf16[1,4,256,128]{3,2,1,0:T(8,128)(2,1)S(1)}, f32[4,8,128]{2,1,0:T(8,128)S(1)}, bf16[8,4,256,128]{3,2,1,0:T(8,128)(2,1)S(1)}, bf16[1024,256]{1,0:T(8,128)(2,1)S(1)}, f32[2,256,128]{2,1,0:T(8,128)S(1)}) custom-call(s32[1,8]{1,0:T(1,128)} %shift_ref.5, f32[1,8]{1,0:T(1,128)} %frac_ref.5, s32[128]{0:T(128)} %valid_ref.7, ...), custom_call_target="tpu_custom_call" | custom-call | tf_op jit(solution)/shard_map/load/pallas_call | solution.py:292
  3.0 0.0 copy-done
  3.0 0.0 copy-done.2
  3.1 0.0 copy-done.1
  3.1 1.8 %shard_map.64 = (bf16[2,4,256,128]{3,2,1,0:T(8,128)(2,1)S(1)}, f32[4,8,128]{2,1,0:T(8,128)S(1)}) custom-call(s32[1,8]{1,0:T(1,128)S(1)} %copy-done.1, f32[1,8]{1,0:T(1,128)S(1)} %copy-done.2, s32[128]{0:T(128)S(1)} %copy-done, bf16[8,4,256,128]{3,2,1,0:T(8,128)(2,1)S(1)} %get-tuple-element.17.img_ref, bf16[1024,256]{1,0:T(8,128)(2,1)S(1)} %get-tuple-element.18.plane_ref, ...), custom_call_target="tpu_custom_call" | custom-call | tf_op jit(solution)/shard_map/pallas_call | solution.py:330
  4.9 3.0 %collective-permute-start.8 = (bf16[2,4,256,128]{3,2,1,0:T(8,128)(2,1)S(1)}, bf16[2,4,256,128]{3,2,1,0:T(8,128)(2,1)S(1)}, u32[]{:S(2)}, u32[]{:S(2)}) collective-permute-start(bf16[2,4,256,128]{3,2,1,0:T(8,128)(2,1)S(1)} %get-tuple-element.27), channel_id=1, source_target_pairs={{0,16},{16,0},{1,17},{17,1},{2,18},{18,2},{3,19},{19,3},{4,20},{20... | collective-permute-start | bytes 1572872 | tf_op jit(solution)/shard_map/ppermute | solution.py:310
  7.9 0.7 %pack.1 = (bf16[256,128]{1,0:T(8,128)(2,1)S(1)}, bf16[256,128]{1,0:T(8,128)(2,1)S(1)}) custom-call(s32[128]{0:T(128)S(1)} %copy-done, bf16[8,4,256,128]{3,2,1,0:T(8,128)(2,1)S(1)} %get-tuple-element.17.img_ref), custom_call_target="tpu_custom_call" | custom-call | tf_op jit(solution)/shard_map/pack/pallas_call | solution.py:315
  8.7 1.5 %collective-permute-start = (bf16[256,128]{1,0:T(8,128)(2,1)S(1)}, bf16[256,128]{1,0:T(8,128)(2,1)S(1)}, u32[]{:S(2)}, u32[]{:S(2)}) collective-permute-start(bf16[256,128]{1,0:T(8,128)(2,1)S(1)} %get-tuple-element.22), channel_id=1, source_target_pairs={{0,1},{1,2},{2,3},{3,4},{4,5},{5,6},{6,7},{7,8},{8,9},{9,10},{10,1... | collective-permute-start | bytes 196616 | tf_op jit(solution)/shard_map/ppermute | solution.py:324
  10.1 1.3 %collective-permute-start.1 = (bf16[256,128]{1,0:T(8,128)(2,1)S(1)}, bf16[256,128]{1,0:T(8,128)(2,1)S(1)}, u32[]{:S(2)}, u32[]{:S(2)}) collective-permute-start(bf16[256,128]{1,0:T(8,128)(2,1)S(1)} %get-tuple-element.23), channel_id=1, source_target_pairs={{1,0},{2,1},{3,2},{4,3},{5,4},{6,5},{7,6},{8,7},{9,8},{10,9},{11,1... | collective-permute-start | bytes 196616 | tf_op jit(solution)/shard_map/ppermute | solution.py:325
  11.4 0.4 collective-permute-start.7
  11.8 0.0 collective-permute-done.refs_0_
  11.8 3.1 %collective-permute-done.1.refs_1_ = bf16[256,128]{1,0:T(8,128)(2,1)S(1)} collective-permute-done((bf16[256,128]{1,0:T(8,128)(2,1)S(1)}, bf16[256,128]{1,0:T(8,128)(2,1)S(1)}, u32[]{:S(2)}, u32[]{:S(2)}) %collective-permute-start.1) | collective-permute-done | bytes 65568 | tf_op jit(solution)/shard_map/ppermute | solution.py:325
  14.9 3.6 %shard_map.65 = (bf16[1,4,256,128]{3,2,1,0:T(8,128)(2,1)S(1)}, bf16[4,4,256,128]{3,2,1,0:T(8,128)(2,1)S(1)}, f32[8,128]{1,0:T(8,128)S(1)}) custom-call(s32[1,8]{1,0:T(1,128)S(1)} %copy-done.1, f32[1,8]{1,0:T(1,128)S(1)} %copy-done.2, s32[128]{0:T(128)S(1)} %copy-done, bf16[8,4,256,128]{3,2,1,0:T(8,128)(2,1)S(1)} %get-tuple-element.17.img_ref, ...), custom_call_target="tpu_custom_call" | custom-call | tf_op jit(solution)/shard_map/pallas_call | solution.py:330
  18.5 0.6 %collective-permute-start.9 = (bf16[1,4,256,128]{3,2,1,0:T(8,128)(2,1)S(1)}, bf16[1,4,256,128]{3,2,1,0:T(8,128)(2,1)S(1)}, u32[]{:S(2)}, u32[]{:S(2)}) collective-permute-start(bf16[1,4,256,128]{3,2,1,0:T(8,128)(2,1)S(1)} %get-tuple-element.28), channel_id=1, source_target_pairs={{0,16},{16,0},{1,17},{17,1},{2,18},{18,2},{3,19},{19,3},{4,20},{20... | collective-permute-start | bytes 786440 | tf_op jit(solution)/shard_map/ppermute | solution.py:310
  19.1 2.9 %collective-permute-start.2 = (f32[8,128]{1,0:T(8,128)S(1)}, f32[8,128]{1,0:T(8,128)S(1)}, u32[]{:S(2)}, u32[]{:S(2)}) collective-permute-start(f32[8,128]{1,0:T(8,128)S(1)} %get-tuple-element.25), channel_id=1, source_target_pairs={{0,1},{1,0},{2,3},{3,2},{4,5},{5,4},{6,7},{7,6},{8,9},{9,8},{10,11... | collective-permute-start | bytes 12296 | tf_op jit(solution)/shard_map/ppermute | solution.py:351
  22.0 0.8 %collective-permute-done.2 = f32[8,128]{1,0:T(8,128)S(1)} collective-permute-done((f32[8,128]{1,0:T(8,128)S(1)}, f32[8,128]{1,0:T(8,128)S(1)}, u32[]{:S(2)}, u32[]{:S(2)}) %collective-permute-start.2) | collective-permute-done | bytes 4128 | tf_op jit(solution)/shard_map/ppermute | solution.py:351
  22.8 2.1 %collective-permute-start.3 = (f32[8,128]{1,0:T(8,128)S(1)}, f32[8,128]{1,0:T(8,128)S(1)}, u32[]{:S(2)}, u32[]{:S(2)}) collective-permute-start(f32[8,128]{1,0:T(8,128)S(1)} %add.12), channel_id=1, source_target_pairs={{0,2},{1,3},{2,0},{3,1},{4,6},{5,7},{6,4},{7,5},{8,10},{9,11},{10,... | collective-permute-start | bytes 12296 | tf_op jit(solution)/shard_map/ppermute | solution.py:351
  25.0 1.6 %collective-permute-done.3 = f32[8,128]{1,0:T(8,128)S(1)} collective-permute-done((f32[8,128]{1,0:T(8,128)S(1)}, f32[8,128]{1,0:T(8,128)S(1)}, u32[]{:S(2)}, u32[]{:S(2)}) %collective-permute-start.3) | collective-permute-done | bytes 4128 | tf_op jit(solution)/shard_map/ppermute | solution.py:351
  26.6 1.6 %collective-permute-start.4 = (f32[8,128]{1,0:T(8,128)S(1)}, f32[8,128]{1,0:T(8,128)S(1)}, u32[]{:S(2)}, u32[]{:S(2)}) collective-permute-start(f32[8,128]{1,0:T(8,128)S(1)} %add.13), channel_id=1, source_target_pairs={{0,4},{1,5},{2,6},{3,7},{4,0},{5,1},{6,2},{7,3},{8,12},{9,13},{10,... | collective-permute-start | bytes 12296 | tf_op jit(solution)/shard_map/ppermute | solution.py:351
  28.1 2.0 %collective-permute-done.4 = f32[8,128]{1,0:T(8,128)S(1)} collective-permute-done((f32[8,128]{1,0:T(8,128)S(1)}, f32[8,128]{1,0:T(8,128)S(1)}, u32[]{:S(2)}, u32[]{:S(2)}) %collective-permute-start.4) | collective-permute-done | bytes 4128 | tf_op jit(solution)/shard_map/ppermute | solution.py:351
  30.2 2.6 %collective-permute-start.5 = (f32[8,128]{1,0:T(8,128)S(1)}, f32[8,128]{1,0:T(8,128)S(1)}, u32[]{:S(2)}, u32[]{:S(2)}) collective-permute-start(f32[8,128]{1,0:T(8,128)S(1)} %add.14), channel_id=1, source_target_pairs={{0,8},{1,9},{2,10},{3,11},{4,12},{5,13},{6,14},{7,15},{8,0},{9,1},... | collective-permute-start | bytes 12296 | tf_op jit(solution)/shard_map/ppermute | solution.py:351
  32.8 1.9 %collective-permute-done.5 = f32[8,128]{1,0:T(8,128)S(1)} collective-permute-done((f32[8,128]{1,0:T(8,128)S(1)}, f32[8,128]{1,0:T(8,128)S(1)}, u32[]{:S(2)}, u32[]{:S(2)}) %collective-permute-start.5) | collective-permute-done | bytes 4128 | tf_op jit(solution)/shard_map/ppermute | solution.py:351
  34.7 1.5 %collective-permute-start.6 = (f32[8,128]{1,0:T(8,128)S(1)}, f32[8,128]{1,0:T(8,128)S(1)}, u32[]{:S(2)}, u32[]{:S(2)}) collective-permute-start(f32[8,128]{1,0:T(8,128)S(1)} %add.15.refs_2_), channel_id=1, source_target_pairs={{0,16},{16,0},{1,17},{17,1},{2,18},{18,2},{3,19},{19,3},{4,20},{20... | collective-permute-start | bytes 12296 | tf_op jit(solution)/shard_map/ppermute | solution.py:355
  36.2 2.1 %collective-permute-done.6.refs_3_ = f32[8,128]{1,0:T(8,128)S(1)} collective-permute-done((f32[8,128]{1,0:T(8,128)S(1)}, f32[8,128]{1,0:T(8,128)S(1)}, u32[]{:S(2)}, u32[]{:S(2)}) %collective-permute-start.6) | collective-permute-done | bytes 4128 | tf_op jit(solution)/shard_map/ppermute | solution.py:355
  38.3 0.0 collective-permute-done.7.refs_4_
  38.3 0.0 collective-permute-done.9.refs_6_
  38.3 0.0 collective-permute-done.8.refs_5_
  38.3 2.0 %norm.1 = bf16[2,1,4,4,256,128]{5,4,3,2,1,0:T(8,128)(2,1)} custom-call(s32[1,128]{1,0:T(1,128)S(1)} %bitcast.5, bf16[4,4,256,128]{3,2,1,0:T(8,128)(2,1)S(1)} %get-tuple-element.24.refs_1_, f32[8,128]{1,0:T(8,128)S(1)} %add.15.refs_2_, f32[8,128]{1,0:T(8,128)S(1)} %collective-permute-done.6.refs_3_, ...), custom_call_target="tpu_custom_call" | custom-call | tf_op jit(solution)/shard_map/norm/pallas_call | solution.py:357
  (4 shorter events, 0.0 us)
Async XLA Ops:
  0.0 3.0 %copy-start = (s32[128]{0:T(128)S(1)}, s32[128]{0:T(128)}, u32[]{:S(2)}) copy-start(s32[128]{0:T(128)} %valid_ref.7) | copy-start | bytes 1540
  0.0 3.0 %copy-start.2 = (f32[1,8]{1,0:T(1,128)S(1)}, f32[1,8]{1,0:T(1,128)}, u32[]{:S(2)}) copy-start(f32[1,8]{1,0:T(1,128)} %frac_ref.5) | copy-start | bytes 100
  0.0 3.1 %copy-start.1 = (s32[1,8]{1,0:T(1,128)S(1)}, s32[1,8]{1,0:T(1,128)}, u32[]{:S(2)}) copy-start(s32[1,8]{1,0:T(1,128)} %shift_ref.5) | copy-start | bytes 100
  4.9 33.4 %collective-permute-start.8 = (bf16[2,4,256,128]{3,2,1,0:T(8,128)(2,1)S(1)}, bf16[2,4,256,128]{3,2,1,0:T(8,128)(2,1)S(1)}, u32[]{:S(2)}, u32[]{:S(2)}) collective-permute-start(bf16[2,4,256,128]{3,2,1,0:T(8,128)(2,1)S(1)} %get-tuple-element.27), channel_id=1, source_target_pairs={{0,16},{16,0},{1,17},{17,1},{2,18},{18,2},{3,19},{19,3},{4,20},{20... | collective-permute-start | bytes 1572872 | tf_op jit(solution)/shard_map/ppermute | solution.py:310
  8.7 3.1 %collective-permute-start = (bf16[256,128]{1,0:T(8,128)(2,1)S(1)}, bf16[256,128]{1,0:T(8,128)(2,1)S(1)}, u32[]{:S(2)}, u32[]{:S(2)}) collective-permute-start(bf16[256,128]{1,0:T(8,128)(2,1)S(1)} %get-tuple-element.22), channel_id=1, source_target_pairs={{0,1},{1,2},{2,3},{3,4},{4,5},{5,6},{6,7},{7,8},{8,9},{9,10},{10,1... | collective-permute-start | bytes 196616 | tf_op jit(solution)/shard_map/ppermute | solution.py:324
  10.1 4.7 %collective-permute-start.1 = (bf16[256,128]{1,0:T(8,128)(2,1)S(1)}, bf16[256,128]{1,0:T(8,128)(2,1)S(1)}, u32[]{:S(2)}, u32[]{:S(2)}) collective-permute-start(bf16[256,128]{1,0:T(8,128)(2,1)S(1)} %get-tuple-element.23), channel_id=1, source_target_pairs={{1,0},{2,1},{3,2},{4,3},{5,4},{6,5},{7,6},{8,7},{9,8},{10,9},{11,1... | collective-permute-start | bytes 196616 | tf_op jit(solution)/shard_map/ppermute | solution.py:325
  11.4 26.9 %collective-permute-start.7 = (bf16[1,4,256,128]{3,2,1,0:T(8,128)(2,1)S(1)}, bf16[1,4,256,128]{3,2,1,0:T(8,128)(2,1)S(1)}, u32[]{:S(2)}, u32[]{:S(2)}) collective-permute-start(bf16[1,4,256,128]{3,2,1,0:T(8,128)(2,1)S(1)} %get-tuple-element.26), channel_id=1, source_target_pairs={{0,16},{16,0},{1,17},{17,1},{2,18},{18,2},{3,19},{19,3},{4,20},{20... | collective-permute-start | bytes 786440 | tf_op jit(solution)/shard_map/ppermute | solution.py:310
  18.5 19.8 %collective-permute-start.9 = (bf16[1,4,256,128]{3,2,1,0:T(8,128)(2,1)S(1)}, bf16[1,4,256,128]{3,2,1,0:T(8,128)(2,1)S(1)}, u32[]{:S(2)}, u32[]{:S(2)}) collective-permute-start(bf16[1,4,256,128]{3,2,1,0:T(8,128)(2,1)S(1)} %get-tuple-element.28), channel_id=1, source_target_pairs={{0,16},{16,0},{1,17},{17,1},{2,18},{18,2},{3,19},{19,3},{4,20},{20... | collective-permute-start | bytes 786440 | tf_op jit(solution)/shard_map/ppermute | solution.py:310
  19.1 3.8 %collective-permute-start.2 = (f32[8,128]{1,0:T(8,128)S(1)}, f32[8,128]{1,0:T(8,128)S(1)}, u32[]{:S(2)}, u32[]{:S(2)}) collective-permute-start(f32[8,128]{1,0:T(8,128)S(1)} %get-tuple-element.25), channel_id=1, source_target_pairs={{0,1},{1,0},{2,3},{3,2},{4,5},{5,4},{6,7},{7,6},{8,9},{9,8},{10,11... | collective-permute-start | bytes 12296 | tf_op jit(solution)/shard_map/ppermute | solution.py:351
  22.8 3.7 %collective-permute-start.3 = (f32[8,128]{1,0:T(8,128)S(1)}, f32[8,128]{1,0:T(8,128)S(1)}, u32[]{:S(2)}, u32[]{:S(2)}) collective-permute-start(f32[8,128]{1,0:T(8,128)S(1)} %add.12), channel_id=1, source_target_pairs={{0,2},{1,3},{2,0},{3,1},{4,6},{5,7},{6,4},{7,5},{8,10},{9,11},{10,... | collective-permute-start | bytes 12296 | tf_op jit(solution)/shard_map/ppermute | solution.py:351
  26.6 3.6 %collective-permute-start.4 = (f32[8,128]{1,0:T(8,128)S(1)}, f32[8,128]{1,0:T(8,128)S(1)}, u32[]{:S(2)}, u32[]{:S(2)}) collective-permute-start(f32[8,128]{1,0:T(8,128)S(1)} %add.13), channel_id=1, source_target_pairs={{0,4},{1,5},{2,6},{3,7},{4,0},{5,1},{6,2},{7,3},{8,12},{9,13},{10,... | collective-permute-start | bytes 12296 | tf_op jit(solution)/shard_map/ppermute | solution.py:351
  30.2 4.5 %collective-permute-start.5 = (f32[8,128]{1,0:T(8,128)S(1)}, f32[8,128]{1,0:T(8,128)S(1)}, u32[]{:S(2)}, u32[]{:S(2)}) collective-permute-start(f32[8,128]{1,0:T(8,128)S(1)} %add.14), channel_id=1, source_target_pairs={{0,8},{1,9},{2,10},{3,11},{4,12},{5,13},{6,14},{7,15},{8,0},{9,1},... | collective-permute-start | bytes 12296 | tf_op jit(solution)/shard_map/ppermute | solution.py:351
  34.7 3.6 %collective-permute-start.6 = (f32[8,128]{1,0:T(8,128)S(1)}, f32[8,128]{1,0:T(8,128)S(1)}, u32[]{:S(2)}, u32[]{:S(2)}) collective-permute-start(f32[8,128]{1,0:T(8,128)S(1)} %add.15.refs_2_), channel_id=1, source_target_pairs={{0,16},{16,0},{1,17},{17,1},{2,18},{18,2},{3,19},{19,3},{4,20},{20... | collective-permute-start | bytes 12296 | tf_op jit(solution)/shard_map/ppermute | solution.py:355
